TPU v7x, 32 devices: a whole 2x2x4 slice. The times are simulated.
32 devices in a mesh: grp: 2 (over y), mon: 4 (over z), pair: 2 (over x), sub: 2 (over core).
Axes of the slice: x: 2, y: 2, z: 4, core: 2. Of those that a mesh axis runs over, the one named last changes fastest.
Arguments:
- dfactors: bfloat16 [8192, 1024], P('mon', 'sub'), may hold values from -0.5 to 0.5
- block_mask: int32 [64, 1024], P('mon', 'sub'), may hold values 0 or 1
- base_flow: float32 [8192], P('mon'), may hold values from -5 to 5
- branch_row: int32 [1024], replicated, may hold values from 0 to 8191, as said below
- pair_slots: int32 [3072, 2], P(('grp', 'pair')), parts along dimension 0, may hold values from 0 to 1023, as said below
- pair_counts: int32 [4], P(('grp', 'pair')), parts along dimension 0, may hold values from 1 to 768, 1024 in all
Outputs:
- post_flows: bfloat16 [8192, 3072], P(('mon', 'sub'), ('grp', 'pair')), parts along dimension 1
There are 2 independent parts, one for each index of `grp`. A program takes and returns all parts, laid end to end along the dimension named above; an argument that names none is the same for every part. Nothing has to cross between parts.
Inputs may be any that keep to these rules, and one draw needn't show every extreme that they name: `branch_row`: all entries distinct. `pair_slots`: the two candidates of a slot differ; empty slots hold valid pairs too. `pair_counts`: the counts sum to 1024; an owner's live slots are its first ones.
All inputs are finite; a program needn't handle non-finite values. No bound on the sum of `block_mask` or of `pair_counts` on one device may be relied on, other than what follows from the above.
Results may differ from a plain program's by a relative error of at most 0.004.
Values may be sent and summed in bfloat16 or wider, within the bound.
A program may use at most 64 MiB of HBM per device.

v0:
```python
import jax
import jax.numpy as jnp
from jax import lax
from jax.sharding import PartitionSpec as P

BLOCK = 128


def build_shift(col_first, col_count, first_out, second_out, shift_first, shift_second):
    columns = col_first + jnp.arange(col_count, dtype=jnp.int32)[:, None]
    return (
        jnp.where(columns == first_out[None, :], shift_first[None, :], jnp.float32(0.0))
        + jnp.where(columns == second_out[None, :], shift_second[None, :], jnp.float32(0.0))
    ).astype(jnp.bfloat16)


def on_device(dfactors, block_mask, base_flow, branch_row, pair_slots, pair_counts):
    rows_dev, col_width = dfactors.shape
    blocks = block_mask.shape[0]
    masked = (
        dfactors.reshape(blocks, BLOCK, col_width) * block_mask.astype(jnp.bfloat16)[:, None, :]
    ).reshape(rows_dev, col_width)
    row_start = lax.axis_index("mon") * rows_dev
    sub_index = lax.axis_index("sub")
    col_start = sub_index * col_width
    sub_count = lax.axis_size("sub")
    capacity = pair_slots.shape[0]
    own_count = pair_counts[0]
    live_slot = (jnp.arange(capacity, dtype=jnp.int32) < own_count).astype(jnp.float32)
    first_out = pair_slots[:, 0]
    second_out = pair_slots[:, 1]
    first_row = branch_row[first_out]
    second_row = branch_row[second_out]

    def entry(row_ids, col_ids):
        local_row = row_ids - row_start
        local_col = col_ids - col_start
        inside = (
            (local_row >= 0) & (local_row < rows_dev) & (local_col >= 0) & (local_col < col_width)
        )
        value = masked[jnp.clip(local_row, 0, rows_dev - 1), jnp.clip(local_col, 0, col_width - 1)]
        return jnp.where(inside, value.astype(jnp.float32), jnp.float32(0.0))

    def flow_part(row_ids):
        local_row = row_ids - row_start
        inside = (local_row >= 0) & (local_row < rows_dev) & (sub_index == 0)
        return jnp.where(inside, base_flow[jnp.clip(local_row, 0, rows_dev - 1)], jnp.float32(0.0))

    cross_pair = jnp.stack([entry(first_row, second_out), entry(second_row, first_out)], axis=1)
    flow_pair = jnp.stack([flow_part(first_row), flow_part(second_row)], axis=1)
    cross_sum, flow_sum = lax.psum((cross_pair, flow_pair), ("mon", "sub"))
    cross_first = cross_sum[:, 0]
    cross_second = cross_sum[:, 1]
    flow_first = flow_sum[:, 0]
    flow_second = flow_sum[:, 1]
    determinant = 1.0 - cross_first * cross_second
    shift_first = (flow_first + cross_first * flow_second) / determinant
    shift_second = (flow_second + cross_second * flow_first) / determinant
    my_rows = rows_dev // sub_count
    shift = build_shift(col_start, col_width, first_out, second_out, shift_first, shift_second)
    delta = lax.psum_scatter(
        jnp.dot(masked, shift, preferred_element_type=jnp.float32).astype(jnp.bfloat16),
        "sub",
        scatter_dimension=0,
        tiled=True,
    ).astype(jnp.float32)
    flows_half = lax.dynamic_slice_in_dim(base_flow, sub_index * my_rows, my_rows, 0)
    post_flow = flows_half[:, None] + delta
    return (post_flow * live_slot[None, :]).astype(jnp.bfloat16)


def solution(mesh):
    return jax.shard_map(
        on_device,
        mesh=mesh,
        in_specs=(
            P("mon", "sub"),
            P("mon", "sub"),
            P("mon"),
            P(),
            P(("grp", "pair"), None),
            P(("grp", "pair")),
        ),
        out_specs=P(("mon", "sub"), ("grp", "pair")),
        check_vma=False,
    )
```

profile of v0, /device:TPU:0, one launch (start us, length us, event | category | flops | bytes accessed | tf_op | source)
XLA Modules:
  0.0 91.6 jit_solution(11011245030587319538)
XLA Ops:
  6.5 0.0 copy-start
  6.5 0.0 reduce-scatter.2.cloned.1.call-start
  6.5 0.7 fusion.14
  7.3 0.0 copy-done
  7.3 0.0 copy-start.2
  7.3 3.2 %gather_fusion.2 = s32[768]{0:T(1024)S(1)} fusion(s32[1024]{0:T(1024)S(1)} %copy-done, s32[1024]{0:T(1024)S(1)} %pad_clamp_fusion.1), kind=kCustom, calls=%fused_computation.2 | custom fusion | bytes 9216 | tf_op jit(solution)/shard_map/gather | solution.py:33
  10.5 0.0 copy-done.2
  10.5 0.1 slice_reduce_fusion.5
  10.6 0.0 copy-start.3
  10.6 3.2 %gather_fusion = s32[768]{0:T(1024)S(1)} fusion(s32[1024]{0:T(1024)S(1)} %copy-done, s32[1024]{0:T(1024)S(1)} %pad_clamp_fusion.3), kind=kCustom, calls=%fused_computation | custom fusion | bytes 9216 | tf_op jit(solution)/shard_map/gather | solution.py:32
  13.9 0.0 copy-done.3
  13.9 1.7 %bitcast_multiply_fusion = bf16[2048,512]{1,0:T(8,128)(2,1)S(1)} fusion(bf16[2048,512]{1,0:T(8,128)(2,1)} %param.6, bf16[16,512]{1,0:T(8,128)(2,1)S(1)} %convert_element_type.48), kind=kLoop, calls=%fused_computation.8 | loop fusion | flops 1048576 | bytes 4210688 | tf_op jit(solution)/shard_map/mul | solution.py:21
  15.7 0.0 copy-start.1
  15.7 6.7 %gather_fusion.4 = bf16[768]{0:T(1024)(128)(2,1)S(1)} fusion(bf16[2048,512]{1,0:T(8,128)(2,1)S(1)} %bitcast_multiply_fusion, s32[768]{0:T(1024)S(1)} %get-tuple-element.14), kind=kCustom, calls=%fused_computation.4 | custom fusion | bytes 9216 | tf_op jit(solution)/shard_map/gather | solution.py:41
  22.5 6.7 %gather_fusion.5 = bf16[768]{0:T(1024)(128)(2,1)S(1)} fusion(bf16[2048,512]{1,0:T(8,128)(2,1)S(1)} %bitcast_multiply_fusion, s32[768]{0:T(1024)S(1)} %get-tuple-element.6), kind=kCustom, calls=%fused_computation.5 | custom fusion | bytes 9216 | tf_op jit(solution)/shard_map/gather | solution.py:41
  29.2 0.0 copy-done.1
  29.2 4.5 %gather_fusion.1 = f32[768]{0:T(1024)S(1)} fusion(f32[2048]{0:T(1024)S(1)} %copy-done.1, s32[1024]{0:T(1024)S(1)} %pad_clamp_fusion.2), kind=kCustom, calls=%fused_computation.1 | custom fusion | bytes 9216 | tf_op jit(solution)/shard_map/gather | solution.py:47
  33.7 4.5 %gather_fusion.3 = f32[768]{0:T(1024)S(1)} fusion(f32[2048]{0:T(1024)S(1)} %copy-done.1, s32[1024]{0:T(1024)S(1)} %pad_clamp_fusion), kind=kCustom, calls=%fused_computation.3 | custom fusion | bytes 9216 | tf_op jit(solution)/shard_map/gather | solution.py:47
  38.3 30.3 %all-reduce = (f32[768,2]{0,1:T(2,128)S(1)}, f32[768,2]{0,1:T(2,128)S(1)}) all-reduce(f32[768,2]{0,1:T(2,128)S(1)} %pad_maximum_fusion, f32[768,2]{0,1:T(2,128)S(1)} %pad_maximum_fusion.1), channel_id=1, replica_groups=mesh['grp'=2,'mon'=4,'pair'=2,'sub'=2] {'mon','sub'}, use_global_device_ids=true, to_apply=%region_0.1 | all-reduce | flops 3072 | bytes 24576 | tf_op jit(solution)/shard_map/psum | solution.py:51
  68.6 3.6 %convolution_convert_fusion = bf16[2048,768]{1,0:T(8,128)(2,1)} fusion(bf16[2048,512]{1,0:T(8,128)(2,1)S(1)} %bitcast_multiply_fusion, f32[768]{0:T(1024)S(1)} %get-tuple-element.19, s32[768]{0:T(1024)S(1)} %get-tuple-element.8, f32[768]{0:T(1024)S(1)} %get-tuple-element.18, s32[768]{0:T(1024)S(1)} %get-tuple-element.5, s32[512]{0:T(512)S(1)} %iota_add_fusion), kind=kOutput, calls=%fused_computation.6 | convolution fusion | flops 1614544896 | bytes 5257216 | tf_op jit(solution)/shard_map/dot_general | solution.py:62
  72.2 0.0 reduce-scatter.2.cloned.1.call-update
  73.0 8.9 %reduce-scatter.2.cloned.1.call-done = bf16[1024,768]{1,0:T(8,128)(2,1)} async-done(((bf16[2048,768]{1,0:T(8,128)(2,1)}), bf16[1024,768]{1,0:T(8,128)(2,1)}) %reduce-scatter.2.cloned.1.call-update) | async-done | bytes 1572880 | tf_op jit(solution)/shard_map/reduce_scatter | solution.py:61
  81.8 3.0 %multiply_convert_fusion = bf16[1024,768]{1,0:T(8,128)(2,1)} fusion(bf16[1024,768]{1,0:T(8,128)(2,1)} %reduce-scatter.2.cloned.1.call-done, f32[768]{0:T(1024)S(1)} %fusion.12, f32[1024]{0:T(1024)S(1)} %dynamic_slice.3), kind=kLoop, calls=%fused_computation.7 | loop fusion | flops 3145728 | bytes 3152896 | tf_op jit(solution)/shard_map/convert_element_type | solution.py:69
  (20 shorter events, 0.2 us)
Async XLA Ops:
  6.5 0.8 copy-start
  6.5 75.3 %reduce-scatter.2.cloned.1.call-start = ((), (), s32[]{:S(2)}) async-start(), calls=%async_computation.1 | async-start | bytes 4718592 | tf_op jit(solution)/shard_map/reduce_scatter | solution.py:61
  7.3 3.2 %copy-start.2 = (s32[768,2]{0,1:T(2,128)S(1)}, s32[768,2]{0,1:T(2,128)}, u32[]{:S(2)}) copy-start(s32[768,2]{0,1:T(2,128)} %param.10) | copy-start | bytes 18436
  10.6 3.3 %copy-start.3 = (s32[16,512]{1,0:T(8,128)S(1)}, s32[16,512]{1,0:T(8,128)}, u32[]{:S(2)}) copy-start(s32[16,512]{1,0:T(8,128)} %param.7) | copy-start | bytes 98308
  15.7 13.6 %copy-start.1 = (f32[2048]{0:T(1024)S(1)}, f32[2048]{0:T(1024)}, u32[]{:S(2)}) copy-start(f32[2048]{0:T(1024)} %param.8) | copy-start | bytes 24580
Sparse Core Ops, SparseCore 0:
  72.4 9.3 reduce-scatter.1
where the time goes:
time: 91.9 us; the launch traced here: 91.6 us
  blocking collectives  30.3 us (33%)
  local copies, waits for them, and re-layouts  28.9 us (31%)
  between operations  14.3 us (16%)
  waiting for transfers between devices  8.88 us (10%)
  other arithmetic  5.66 us (6%)
  matrix products  3.63 us (4%)
    psum x1, blocking collectives, on_device(): cross_sum, flow_sum = lax.psum((cross_pair, flow_pair), ('mon', 'sub'))  30.3 us
    gather x2, local copies, waits for them, and re-layouts, entry(): masked[jnp.clip(local_row, 0, rows_dev - 1), jnp.clip(local_col, 0, col_w...  13.5 us
    gather x2, local copies, waits for them, and re-layouts, flow_part(): base_flow[jnp.clip(local_row, 0, rows_dev - 1)]  8.93 us
    reduce_scatter x1, waiting for transfers between devices, on_device(): lax.psum_scatter(jnp.dot(masked, shift, preferred_element_type=jnp.float3...  8.86 us
    dot_general x1, matrix products, on_device(): jnp.dot(masked, shift, preferred_element_type=jnp.float32)  3.63 us
    gather x1, local copies, waits for them, and re-layouts, on_device(): second_row = branch_row[second_out]  3.19 us
    gather x1, local copies, waits for them, and re-layouts, on_device(): first_row = branch_row[first_out]  3.19 us
    convert_element_type x1, other arithmetic, on_device(): return (post_flow * live_slot[None, :]).astype(jnp.bfloat16)  2.98 us
  transfers between devices with their start and end apart: 1, of which 1 were waited for; matrix products, arithmetic and copies ran while one was open for 0% of the time, Pallas kernels for 0%

commit v1 on v0

--- a/solution.py
+++ b/solution.py
@@ -4,6 +4,11 @@
 from jax.sharding import PartitionSpec as P
 
 BLOCK = 128
+
+
+def axis_by_axis(value_2, first, second):
+    partial = lax.psum(value_2, first)
+    return lax.psum(partial, second)
 
 
 def build_shift(col_first, col_count, first_out, second_out, shift_first, shift_second):
@@ -48,7 +53,7 @@
 
     cross_pair = jnp.stack([entry(first_row, second_out), entry(second_row, first_out)], axis=1)
     flow_pair = jnp.stack([flow_part(first_row), flow_part(second_row)], axis=1)
-    cross_sum, flow_sum = lax.psum((cross_pair, flow_pair), ("mon", "sub"))
+    cross_sum, flow_sum = axis_by_axis((cross_pair, flow_pair), "sub", "mon")
     cross_first = cross_sum[:, 0]
     cross_second = cross_sum[:, 1]
     flow_first = flow_sum[:, 0]

time: 91.9 us -> 85.3 us (0.928)
  blocking collectives: 30.3 us -> 23.7 us
    psum x1 -> x2, blocking collectives: 30.3 us -> 23.7 us  [the longest x1 20.1 us: axis_by_axis(): return lax.psum(partial, second)]
where the time goes in v1:
time: 85.3 us; the launch traced here: 85.1 us
  local copies, waits for them, and re-layouts  28.9 us (34%)
  blocking collectives  23.7 us (28%)
  between operations  14.3 us (17%)
  waiting for transfers between devices  8.88 us (10%)
  other arithmetic  5.66 us (7%)
  matrix products  3.63 us (4%)
    psum x1, blocking collectives, axis_by_axis(): return lax.psum(partial, second)  20.1 us
    gather x2, local copies, waits for them, and re-layouts, entry(): masked[jnp.clip(local_row, 0, rows_dev - 1), jnp.clip(local_col, 0, col_w...  13.5 us
    gather x2, local copies, waits for them, and re-layouts, flow_part(): base_flow[jnp.clip(local_row, 0, rows_dev - 1)]  8.93 us
    reduce_scatter x1, waiting for transfers between devices, on_device(): lax.psum_scatter(jnp.dot(masked, shift, preferred_element_type=jnp.float3...  8.86 us
    dot_general x1, matrix products, on_device(): jnp.dot(masked, shift, preferred_element_type=jnp.float32)  3.63 us
    psum x1, blocking collectives, axis_by_axis(): partial = lax.psum(value_2, first)  3.61 us
    gather x1, local copies, waits for them, and re-layouts, on_device(): second_row = branch_row[second_out]  3.19 us
    gather x1, local copies, waits for them, and re-layouts, on_device(): first_row = branch_row[first_out]  3.19 us
  transfers between devices with their start and end apart: 1, of which 1 were waited for; matrix products, arithmetic and copies ran while one was open for 0% of the time, Pallas kernels for 0%

profile of v1, /device:TPU:0, one launch (start us, length us, event | category | flops | bytes accessed | tf_op | source)
XLA Modules:
  0.0 85.1 jit_solution(1601626189836373448)
XLA Ops:
  6.5 0.0 copy-start
  6.5 0.0 reduce-scatter.2.cloned.1.call-start
  6.5 0.7 fusion.14
  7.3 0.0 copy-done
  7.3 0.0 copy-start.2
  7.3 3.2 %gather_fusion.2 = s32[768]{0:T(1024)S(1)} fusion(s32[1024]{0:T(1024)S(1)} %copy-done, s32[1024]{0:T(1024)S(1)} %pad_clamp_fusion.1), kind=kCustom, calls=%fused_computation.2 | custom fusion | bytes 9216 | tf_op jit(solution)/shard_map/gather | solution.py:38
  10.5 0.0 copy-done.2
  10.5 0.1 slice_reduce_fusion.5
  10.6 0.0 copy-start.3
  10.6 3.2 %gather_fusion = s32[768]{0:T(1024)S(1)} fusion(s32[1024]{0:T(1024)S(1)} %copy-done, s32[1024]{0:T(1024)S(1)} %pad_clamp_fusion.3), kind=kCustom, calls=%fused_computation | custom fusion | bytes 9216 | tf_op jit(solution)/shard_map/gather | solution.py:37
  13.9 0.0 copy-done.3
  13.9 1.7 %bitcast_multiply_fusion = bf16[2048,512]{1,0:T(8,128)(2,1)S(1)} fusion(bf16[2048,512]{1,0:T(8,128)(2,1)} %param.6, bf16[16,512]{1,0:T(8,128)(2,1)S(1)} %convert_element_type.48), kind=kLoop, calls=%fused_computation.8 | loop fusion | flops 1048576 | bytes 4210688 | tf_op jit(solution)/shard_map/mul | solution.py:26
  15.7 0.0 copy-start.1
  15.7 6.7 %gather_fusion.4 = bf16[768]{0:T(1024)(128)(2,1)S(1)} fusion(bf16[2048,512]{1,0:T(8,128)(2,1)S(1)} %bitcast_multiply_fusion, s32[768]{0:T(1024)S(1)} %get-tuple-element.14), kind=kCustom, calls=%fused_computation.4 | custom fusion | bytes 9216 | tf_op jit(solution)/shard_map/gather | solution.py:46
  22.5 6.7 %gather_fusion.5 = bf16[768]{0:T(1024)(128)(2,1)S(1)} fusion(bf16[2048,512]{1,0:T(8,128)(2,1)S(1)} %bitcast_multiply_fusion, s32[768]{0:T(1024)S(1)} %get-tuple-element.6), kind=kCustom, calls=%fused_computation.5 | custom fusion | bytes 9216 | tf_op jit(solution)/shard_map/gather | solution.py:46
  29.2 0.0 copy-done.1
  29.2 4.5 %gather_fusion.1 = f32[768]{0:T(1024)S(1)} fusion(f32[2048]{0:T(1024)S(1)} %copy-done.1, s32[1024]{0:T(1024)S(1)} %pad_clamp_fusion.2), kind=kCustom, calls=%fused_computation.1 | custom fusion | bytes 9216 | tf_op jit(solution)/shard_map/gather | solution.py:52
  33.7 4.5 %gather_fusion.3 = f32[768]{0:T(1024)S(1)} fusion(f32[2048]{0:T(1024)S(1)} %copy-done.1, s32[1024]{0:T(1024)S(1)} %pad_clamp_fusion), kind=kCustom, calls=%fused_computation.3 | custom fusion | bytes 9216 | tf_op jit(solution)/shard_map/gather | solution.py:52
  38.3 3.6 %all-reduce.1 = (f32[768,2]{0,1:T(2,128)S(1)}, f32[768,2]{0,1:T(2,128)S(1)}) all-reduce(f32[768,2]{0,1:T(2,128)S(1)} %pad_maximum_fusion, f32[768,2]{0,1:T(2,128)S(1)} %pad_maximum_fusion.1), channel_id=1, replica_groups=mesh['grp'=2,'mon'=4,'pair'=2,'sub'=2] {'sub'}, use_global_device_ids=true, to_apply=%region_0.1 | all-reduce | flops 3072 | bytes 24576 | tf_op jit(solution)/shard_map/psum | solution.py:10
  41.9 20.1 %all-reduce = (f32[768,2]{0,1:T(2,128)S(1)}, f32[768,2]{0,1:T(2,128)S(1)}) all-reduce(f32[768,2]{0,1:T(2,128)S(1)} %get-tuple-element.18, f32[768,2]{0,1:T(2,128)S(1)} %get-tuple-element.19), channel_id=1, replica_groups=mesh['grp'=2,'mon'=4,'pair'=2,'sub'=2] {'mon'}, use_global_device_ids=true, to_apply=%region_1.2 | all-reduce | flops 3072 | bytes 24576 | tf_op jit(solution)/shard_map/psum | solution.py:11
  62.0 3.6 %convolution_convert_fusion = bf16[2048,768]{1,0:T(8,128)(2,1)} fusion(bf16[2048,512]{1,0:T(8,128)(2,1)S(1)} %bitcast_multiply_fusion, f32[768]{0:T(1024)S(1)} %get-tuple-element.21, s32[768]{0:T(1024)S(1)} %get-tuple-element.8, f32[768]{0:T(1024)S(1)} %get-tuple-element.20, s32[768]{0:T(1024)S(1)} %get-tuple-element.5, s32[512]{0:T(512)S(1)} %iota_add_fusion), kind=kOutput, calls=%fused_computation.6 | convolution fusion | flops 1614544896 | bytes 5257216 | tf_op jit(solution)/shard_map/dot_general | solution.py:67
  65.7 0.0 reduce-scatter.2.cloned.1.call-update
  66.4 8.9 %reduce-scatter.2.cloned.1.call-done = bf16[1024,768]{1,0:T(8,128)(2,1)} async-done(((bf16[2048,768]{1,0:T(8,128)(2,1)}), bf16[1024,768]{1,0:T(8,128)(2,1)}) %reduce-scatter.2.cloned.1.call-update) | async-done | bytes 1572880 | tf_op jit(solution)/shard_map/reduce_scatter | solution.py:66
  75.2 3.0 %multiply_convert_fusion = bf16[1024,768]{1,0:T(8,128)(2,1)} fusion(bf16[1024,768]{1,0:T(8,128)(2,1)} %reduce-scatter.2.cloned.1.call-done, f32[768]{0:T(1024)S(1)} %fusion.12, f32[1024]{0:T(1024)S(1)} %dynamic_slice.3), kind=kLoop, calls=%fused_computation.7 | loop fusion | flops 3145728 | bytes 3152896 | tf_op jit(solution)/shard_map/convert_element_type | solution.py:74
  (20 shorter events, 0.2 us)
Async XLA Ops:
  6.5 0.8 copy-start
  6.5 68.7 %reduce-scatter.2.cloned.1.call-start = ((), (), s32[]{:S(2)}) async-start(), calls=%async_computation.1 | async-start | bytes 4718592 | tf_op jit(solution)/shard_map/reduce_scatter | solution.py:66
  7.3 3.2 %copy-start.2 = (s32[768,2]{0,1:T(2,128)S(1)}, s32[768,2]{0,1:T(2,128)}, u32[]{:S(2)}) copy-start(s32[768,2]{0,1:T(2,128)} %param.10) | copy-start | bytes 18436
  10.6 3.3 %copy-start.3 = (s32[16,512]{1,0:T(8,128)S(1)}, s32[16,512]{1,0:T(8,128)}, u32[]{:S(2)}) copy-start(s32[16,512]{1,0:T(8,128)} %param.7) | copy-start | bytes 98308
  15.7 13.6 %copy-start.1 = (f32[2048]{0:T(1024)S(1)}, f32[2048]{0:T(1024)}, u32[]{:S(2)}) copy-start(f32[2048]{0:T(1024)} %param.8) | copy-start | bytes 24580
Sparse Core Ops, SparseCore 0:
  65.8 9.3 reduce-scatter.1
